TPU v7x, 32 devices: a whole 2x2x4 slice. The times are simulated.
32 devices in a mesh: req: 8 (over z, y), tp: 4 (over x, core).
Axes of the slice: x: 2, y: 2, z: 4, core: 2. Of those that a mesh axis runs over, the one named last changes fastest.
Arguments:
- hidden_in: bfloat16 [512, 2048], P('req'), may hold values from -6 to 6
- queries: bfloat16 [512, 2048], P('req', 'tp'), may hold values from -200 to 200, as said below
- keys_new: bfloat16 [512, 2048], P('req', 'tp'), may hold values from -6 to 6
- values_new: bfloat16 [512, 2048], P('req', 'tp'), may hold values from -6 to 6
- prefix_keys: bfloat16 [8, 16, 2048], P('req', None, 'tp'), may hold values from -6 to 6
- prefix_values: bfloat16 [8, 16, 2048], P('req', None, 'tp'), may hold values from -6 to 6
- block_group: int32 [8], P('req'), may hold values from 0 to 1, as said below
- req_group: int32 [8], P('req'), may hold values from 0 to 1
- lengths: int32 [8], P('req'), may hold values from 1 to 64, 320 in all
- w_out: bfloat16 [2048, 2048], P('tp'), may hold values from -0.125 to 0.125
- norm_gain: bfloat16 [2048], replicated, may hold values from 0.25 to 1.75
- w_router: float32 [2048, 64], replicated, may hold values from -7 to 7
- routes: int32 [512, 8], P('req'), may hold values from 0 to 63, all different within a row; in each aligned block of 64 rows (0 to 63, 64 to 127, ...) at most 10 rows name the same one
- w_gate: bfloat16 [128, 2048, 512], P('req', None, 'tp'), may hold values from -0.125 to 0.125
- w_up: bfloat16 [128, 2048, 512], P('req', None, 'tp'), may hold values from -0.125 to 0.125
- w_down: bfloat16 [128, 512, 2048], P('req', 'tp'), may hold values from -0.1875 to 0.1875
Outputs:
- layer_out: bfloat16 [512, 2048], P('req', 'tp')
Inputs may be any that keep to these rules, and one draw needn't show every extreme that they name: queries: the printed draw and the hidden one differ in row scales. `block_group`: exactly half of the 8 cache blocks belong to each group. `routes`: within the rows of one request, each expert is named by at most 10 rows, a bound that some block reaches. `lengths`: each request has at least one live suffix slot, and some request has all 64.
All inputs are finite; a program needn't handle non-finite values. No bound on the sum of `lengths` on one device may be relied on, other than what follows from the above.
Results may differ from a plain program's by a relative error of at most 0.025.
Values may be sent and summed in bfloat16 or wider, within the bound.
A program may use at most 128 MiB of HBM per device.

v0:
```python
import math

import jax
import jax.numpy as jnp
from jax import lax
from jax.sharding import PartitionSpec as P

HD = 128
E = 64
TOPK = 8
CAP = 10


epsilon = 1e-06


def slot_numbers(block_routes):
    flatten = block_routes.reshape(-1)
    chosen = (flatten[:, None] == jnp.arange(E, dtype=jnp.int32)[None, :]).astype(jnp.int32)
    earlier = jnp.cumsum(chosen, axis=0) - chosen
    return (flatten, jnp.sum(earlier * chosen, axis=1))


def body(
    hidden_in,
    queries,
    keys_new,
    values_new,
    prefix_keys,
    prefix_values,
    block_group,
    req_group,
    lengths,
    w_out,
    norm_gain,
    w_router,
    routes,
    w_gate,
    w_up,
    w_down,
):
    row_count = queries.shape[0]
    local_heads = queries.shape[1] // HD
    width = hidden_in.shape[1]
    factor = 1.0 / math.sqrt(HD)
    query_rows = queries.reshape(row_count, local_heads, HD)
    key_rows = keys_new.reshape(row_count, local_heads, HD)
    value_rows = values_new.reshape(row_count, local_heads, HD)
    group_id = req_group[0].astype(jnp.float32)
    own_valid = jnp.arange(row_count) < lengths[0]
    scores = (
        jnp.einsum("qhd,khd->hqk", query_rows, key_rows, preferred_element_type=jnp.float32)
        * factor
    )
    scores = jnp.where(own_valid[None, None, :], scores, -jnp.inf)
    top_score = jnp.max(scores, axis=-1)
    weights = jnp.exp(scores - top_score[..., None])
    best = top_score
    total = jnp.sum(weights, axis=-1)
    summed = jnp.einsum(
        "hqk,khd->hqd", weights.astype(jnp.bfloat16), value_rows, preferred_element_type=jnp.float32
    )
    piece_keys = lax.all_gather(prefix_keys, "req", axis=0, tiled=True)
    piece_values = lax.all_gather(prefix_values, "req", axis=0, tiled=True)
    piece_groups = lax.all_gather(block_group.astype(jnp.bfloat16), "req", axis=0, tiled=True)
    count = piece_keys.shape[0] * piece_keys.shape[1]
    flat_keys = piece_keys.reshape(count, local_heads, HD)
    flat_values = piece_values.reshape(count, local_heads, HD)
    key_valid = jnp.repeat(piece_groups.astype(jnp.float32), piece_keys.shape[1]) == group_id
    block_scores = (
        jnp.einsum("qhd,khd->hqk", query_rows, flat_keys, preferred_element_type=jnp.float32)
        * factor
    )
    block_scores = jnp.where(key_valid[None, None, :], block_scores, -jnp.inf)
    new_best = jnp.maximum(best, jnp.max(block_scores, axis=-1))
    shrink = jnp.exp(best - new_best)
    block_weights = jnp.exp(block_scores - new_best[..., None])
    added = jnp.einsum(
        "hqk,khd->hqd",
        block_weights.astype(jnp.bfloat16),
        flat_values,
        preferred_element_type=jnp.float32,
    )
    best, total, summed = (
        new_best,
        total * shrink + jnp.sum(block_weights, axis=-1),
        summed * shrink[..., None] + added,
    )
    mixed = (summed / total[..., None]).astype(jnp.bfloat16)
    mixed = jnp.transpose(mixed, (1, 0, 2)).reshape(row_count, local_heads * HD)
    partial_value = jnp.dot(mixed, w_out, preferred_element_type=jnp.float32)
    tp_count = lax.axis_size("tp")
    col_width = width // tp_count
    col_start = lax.axis_index("tp") * col_width
    whole = hidden_in.astype(jnp.float32) + lax.psum(
        partial_value.astype(jnp.bfloat16), "tp"
    ).astype(jnp.float32)
    mean_square = jnp.mean(whole * whole, axis=1, keepdims=True)
    normed = (
        whole * lax.rsqrt(mean_square + epsilon) * norm_gain.astype(jnp.float32)[None, :]
    ).astype(jnp.bfloat16)
    state_cols = lax.dynamic_slice_in_dim(whole, col_start, col_width, 1)
    logits = jnp.dot(normed.astype(jnp.float32), w_router, precision=lax.Precision.HIGHEST)
    expert_ids = jnp.arange(E, dtype=jnp.int32)
    picked = jnp.sum(
        jnp.where(routes[:, :, None] == expert_ids[None, None, :], logits[:, None, :], 0.0), axis=2
    )
    gates = jax.nn.softmax(picked, axis=1)
    flatten, slot = slot_numbers(routes)
    position = (flatten * CAP + slot).reshape(row_count, TOPK)
    columns = jnp.arange(E * CAP, dtype=jnp.int32)
    hits = position[:, :, None] == columns[None, None, :]
    placing = jnp.any(hits, axis=1).astype(jnp.bfloat16)
    outgoing = jnp.einsum("tc,td->cd", placing, normed, preferred_element_type=jnp.float32).astype(
        jnp.bfloat16
    )
    combining = jnp.sum(jnp.where(hits, gates[:, :, None], 0.0), axis=1)
    doubled = jnp.repeat(outgoing.reshape(E, CAP, width), 2, axis=0)
    received = lax.all_to_all(doubled, "req", split_axis=0, concat_axis=1, tiled=True)
    gate_val = jnp.einsum("lrd,ldf->lrf", received, w_gate, preferred_element_type=jnp.float32)
    up_val = jnp.einsum("lrd,ldf->lrf", received, w_up, preferred_element_type=jnp.float32)
    inner = (jax.nn.silu(gate_val) * up_val).astype(jnp.bfloat16)
    pieces = jnp.einsum("lrf,lfd->lrd", inner, w_down, preferred_element_type=jnp.float32).astype(
        jnp.bfloat16
    )
    returned = lax.all_to_all(pieces, "req", split_axis=1, concat_axis=0, tiled=True)
    summed_halves = jnp.sum(returned.reshape(E, 2, CAP, width).astype(jnp.float32), axis=1).reshape(
        E * CAP, width
    )
    expert_part = jnp.dot(
        combining,
        summed_halves,
        precision=lax.Precision.HIGHEST,
        preferred_element_type=jnp.float32,
    )
    expert_cols = lax.psum_scatter(
        expert_part.astype(jnp.bfloat16), "tp", scatter_dimension=1, tiled=True
    ).astype(jnp.float32)
    return (state_cols + expert_cols).astype(jnp.bfloat16)


def solution(mesh):
    in_specs = (
        P("req", None),
        P("req", "tp"),
        P("req", "tp"),
        P("req", "tp"),
        P("req", None, "tp"),
        P("req", None, "tp"),
        P("req"),
        P("req"),
        P("req"),
        P("tp", None),
        P(),
        P(),
        P("req", None),
        P("req", None, "tp"),
        P("req", None, "tp"),
        P("req", "tp", None),
    )
    out_specs = P("req", "tp")
    return jax.shard_map(body, mesh=mesh, in_specs=in_specs, out_specs=out_specs, check_vma=False)
```

profile of v0, /device:TPU:0, one launch (start us, length us, event | category | flops | bytes accessed | tf_op | source)
XLA Modules:
  0.0 583.2 jit_solution(14911283072433838208)
XLA Ops:
  8.7 1.2 dynamic-slice
  10.0 0.8 dynamic-update-slice
  10.7 23.1 %all-reduce = bf16[8]{0:T(256)(128)(2,1)S(1)} all-reduce(bf16[8]{0:T(256)(128)(2,1)S(1)} %dynamic-update-slice), channel_id=1, replica_groups=mesh['req'=8,'tp'=4] {'req'}, use_global_device_ids=true, to_apply=%add | all-reduce | flops 8 | bytes 32
  33.9 0.1 eq.67
  34.0 30.7 %all_gather.10 = bf16[8,16,512]{2,1,0:T(8,128)(2,1)S(1)} all-gather(bf16[1,16,512]{2,1,0:T(8,128)(2,1)} %param.20), channel_id=1, replica_groups=mesh['req'=8,'tp'=4] {'req'}, dimensions={0}, use_global_device_ids=true | all-gather | bytes 147456 | tf_op jit(solution)/shard_map/all_gather | solution.py:63
  64.8 30.7 %all_gather.11 = bf16[8,16,512]{2,1,0:T(8,128)(2,1)S(1)} all-gather(bf16[1,16,512]{2,1,0:T(8,128)(2,1)} %param.21), channel_id=1, replica_groups=mesh['req'=8,'tp'=4] {'req'}, dimensions={0}, use_global_device_ids=true | all-gather | bytes 147456 | tf_op jit(solution)/shard_map/all_gather | solution.py:64
  95.5 1.1 fusion.57
  96.7 1.1 fusion.56
  97.8 0.2 fusion.34
  98.0 1.1 fusion.14
  99.1 0.2 fusion.19
  99.3 1.2 convolution_convert_fusion.3
  100.5 0.1 copy.95
  100.6 0.1 eq.72
  100.7 0.1 eq.68
  100.8 1.2 reduce-window.6
  102.0 0.2 slice_reduce_fusion
  102.3 0.1 fusion.28
  102.4 0.1 reduce_sum.83
  102.6 0.1 copy.99
  102.7 0.5 fusion.4
  103.2 26.7 %all-reduce.3.cloned.1.call-done = bf16[64,2048]{1,0:T(8,128)(2,1)} async-done(((bf16[64,2048]{1,0:T(8,128)(2,1)}), bf16[64,2048]{1,0:T(8,128)(2,1)}) %all-reduce.3.cloned.1.call-update) | async-done | bytes 262160 | tf_op jit(solution)/shard_map/psum | solution.py:95
  129.9 1.1 convert_add_fusion
  131.0 3.4 convolution_convert_fusion.1
  134.4 5.4 reshape.145
  139.8 6.8 %broadcast_in_dim.79 = bf16[64,2,10,2048]{3,2,1,0:T(8,128)(2,1)} broadcast(bf16[64,10,2048]{2,1,0:T(8,128)(2,1)} %reshape.145), dimensions={0,2,3} | broadcast | bytes 7864320 | tf_op jit(solution)/shard_map/broadcast_in_dim | solution.py:118
  146.5 187.5 %all_to_all.27 = bf16[128,10,2048]{2,1,0:T(8,128)(2,1)S(1)} all-to-all(bf16[128,10,2048]{2,1,0:T(8,128)(2,1)} %bitcast.107), channel_id=1, replica_groups=mesh['req'=8,'tp'=4] {'req'}, dimensions={0} | all-to-all | bytes 10485760 | tf_op jit(solution)/shard_map/all_to_all | solution.py:119
  334.0 3.4 copy.105
  337.4 2.3 copy-done.2
  339.7 9.7 %fusion.2 = f32[16,80,128]{2,1,0:T(8,128)S(1)} fusion(bf16[16,2048,128]{2,1,0:T(8,128)(2,1)} %param.29, bf16[16,80,2048]{2,0,1:T(8,128)(2,1)S(1)} %bitcast.109), kind=kOutput, calls=%fused_computation.3 | convolution fusion | flops 671088640 | bytes 14286848 | tf_op jit(solution)/shard_map/lrd,ldf->lrf/dot_general | solution.py:120
  349.5 17.3 %convolution_convert_fusion = bf16[16,80,2048]{2,1,0:T(8,128)(2,1)} fusion(bf16[16,128,2048]{2,1,0:T(8,128)(2,1)} %param.31, bf16[16,2048,128]{2,1,0:T(8,128)(2,1)} %param.30, bf16[16,80,2048]{2,0,1:T(8,128)(2,1)} %bitcast.110, f32[16,80,128]{2,1,0:T(8,128)S(1)} %fusion.2), kind=kOutput, calls=%fused_computation.5 | convolution fusion | flops 1345781760 | bytes 27918336 | tf_op jit(solution)/shard_map/lrf,lfd->lrd/dot_general | solution.py:123
  366.8 7.7 %copy.108 = bf16[16,80,2048]{2,0,1:T(8,128)(2,1)} copy(bf16[16,80,2048]{2,1,0:T(8,128)(2,1)} %convolution_convert_fusion) | data formatting | bytes 10485760 | tf_op jit(solution)/shard_map/convert_element_type | solution.py:123
  374.5 4.8 all-to-all-start.1
  379.4 0.5 fusion.54
  379.8 0.2 select_reduce_fusion.1
  380.1 0.1 reduce_max.35
  380.3 0.1 copy.103
  380.4 0.5 select_reduce_fusion
  380.8 113.0 %all-to-all-done.1 = bf16[16,80,2048]{2,0,1:T(8,128)(2,1)} async-done(((bf16[16,80,2048]{2,0,1:T(8,128)(2,1)}), bf16[16,80,2048]{2,0,1:T(8,128)(2,1)}, u32[]{:S(2)}, u32[]{:S(2)}) %all-to-all-start.1) | async-done | bytes 5242912 | tf_op jit(solution)/shard_map/all_to_all | solution.py:126
  493.9 3.9 convert_bitcast_fusion
  497.8 4.7 copy.109
  502.5 13.2 %reshape.148 = f32[64,2,10,2048]{3,1,0,2:T(2,128)} reshape(f32[8,16,10,2048]{3,1,0,2:T(8,128)} %copy.109) | data formatting | bytes 20971520 | tf_op jit(solution)/shard_map/convert_element_type | solution.py:127
  515.6 17.0 %reduce_sum.88 = f32[64,10,2048]{2,0,1:T(8,128)} reduce(f32[64,2,10,2048]{3,1,0,2:T(2,128)} %reshape.148, f32[]{:T(128)} %constant.14.clone.1), dimensions={1}, to_apply=%region_14.15 | reduce | flops 1310720 | bytes 15728644 | tf_op jit(solution)/shard_map/reduce_sum | solution.py:127
  532.6 8.9 %copy.110 = f32[64,10,2048]{2,1,0:T(8,128)} copy(f32[64,10,2048]{2,0,1:T(8,128)} %reduce_sum.88) | data formatting | bytes 10485760 | tf_op jit(solution)/shard_map/reduce_sum | solution.py:127
  541.5 7.6 %reshape.147 = f32[640,2048]{1,0:T(8,128)} reshape(f32[64,10,2048]{2,1,0:T(8,128)} %copy.110) | data formatting | bytes 10485760 | tf_op jit(solution)/shard_map/reshape | solution.py:127
  549.1 6.4 %convolution_convert_fusion.2 = bf16[64,2048]{1,0:T(8,128)(2,1)} fusion(f32[64,640]{1,0:T(8,128)S(1)} %select_reduce_fusion, f32[640,2048]{1,0:T(8,128)} %reshape.147), kind=kOutput, calls=%fused_computation.7 | convolution fusion | flops 1006764032 | bytes 5668864 | tf_op jit(solution)/shard_map/dot_general | solution.py:130
  555.5 18.9 %reduce-scatter.2.cloned.1.call-done = bf16[64,512]{1,0:T(8,128)(2,1)} async-done(((bf16[64,2048]{1,0:T(8,128)(2,1)}), bf16[64,512]{1,0:T(8,128)(2,1)}) %reduce-scatter.2.cloned.1.call-update) | async-done | bytes 65552 | tf_op jit(solution)/shard_map/reduce_scatter | solution.py:136
  574.4 1.5 add_convert_fusion
  (38 shorter events, 0.6 us)
Async XLA Ops:
  6.5 92.8 %copy-start = (bf16[512,2048]{1,0:T(8,128)(2,1)S(1)}, bf16[512,2048]{1,0:T(8,128)(2,1)}, u32[]{:S(2)}) copy-start(bf16[512,2048]{1,0:T(8,128)(2,1)} %param.25) | copy-start | bytes 6291460
  6.5 94.0 %copy-start.6 = (s32[64,8]{0,1:T(8,128)S(1)}, s32[64,8]{0,1:T(8,128)}, u32[]{:S(2)}) copy-start(s32[64,8]{0,1:T(8,128)} %param.28) | copy-start | bytes 6148
  6.5 94.2 %copy-start.7 = (bf16[2048]{0:T(1024)(128)(2,1)S(1)}, bf16[2048]{0:T(1024)(128)(2,1)}, u32[]{:S(2)}) copy-start(bf16[2048]{0:T(1024)(128)(2,1)} %param.26) | copy-start | bytes 12292
  6.5 123.3 %copy-start.3 = (bf16[64,2048]{1,0:T(8,128)(2,1)S(1)}, bf16[64,2048]{1,0:T(8,128)(2,1)}, u32[]{:S(2)}) copy-start(bf16[64,2048]{1,0:T(8,128)(2,1)} %param.16) | copy-start | bytes 786436
  6.5 123.3 %all-reduce.3.cloned.1.call-start = ((), (), s32[]{:S(2)}) async-start(), calls=%async_computation.3 | async-start | bytes 524288 | tf_op jit(solution)/shard_map/psum | solution.py:95
  337.4 2.3 copy-start.2
  374.5 4.9 copy-start.4
  374.5 4.9 copy-start.5
  374.5 119.4 %all-to-all-start.1 = ((bf16[16,80,2048]{2,0,1:T(8,128)(2,1)}), bf16[16,80,2048]{2,0,1:T(8,128)(2,1)}, u32[]{:S(2)}, u32[]{:S(2)}) async-start(bf16[16,80,2048]{2,0,1:T(8,128)(2,1)} %copy.108), calls=%async_computation.1 | async-start | bytes 10485760 | tf_op jit(solution)/shard_map/all_to_all | solution.py:126
  379.3 195.1 %reduce-scatter.2.cloned.1.call-start = ((), (), s32[]{:S(2)}) async-start(), calls=%async_computation.4 | async-start | bytes 327680 | tf_op jit(solution)/shard_map/reduce_scatter | solution.py:136
  541.5 34.4 %copy-start.1 = (bf16[512,2048]{1,0:T(8,128)(2,1)S(1)}, bf16[512,2048]{1,0:T(8,128)(2,1)}, u32[]{:S(2)}) copy-start(bf16[512,2048]{1,0:T(8,128)(2,1)} %param.25) | copy-start | bytes 6291460
Sparse Core Ops, SparseCore 0:
  100.6 29.2 all-reduce.2
  555.6 18.7 reduce-scatter.1
where the time goes:
time: 588 us; the launch traced here: 583 us
  blocking collectives  272 us (46%)
  waiting for transfers between devices  159 us (27%)
  local copies, waits for them, and re-layouts  63 us (11%)
  matrix products  42 us (7%)
  other arithmetic  26.5 us (5%)
  between operations  16.2 us (3%)
    all_to_all x1, blocking collectives, body(): lax.all_to_all(doubled, 'req', split_axis=0, concat_axis=1, tiled=True)  187 us
    all_to_all x1, waiting for transfers between devices, body(): lax.all_to_all(pieces, 'req', split_axis=1, concat_axis=0, tiled=True)  113 us
    all_gather x1, blocking collectives, body(): piece_values = lax.all_gather(prefix_values, 'req', axis=0, tiled=True)  30.7 us
    all_gather x1, blocking collectives, body(): piece_keys = lax.all_gather(prefix_keys, 'req', axis=0, tiled=True)  30.7 us
    psum x1, waiting for transfers between devices, body(): lax.psum(partial_value.astype(jnp.bfloat16), 'tp').astype(jnp.float32)  26.7 us
    unnamed x1, blocking collectives  23.1 us
    reduce_scatter x1, waiting for transfers between devices, body(): lax.psum_scatter(expert_part.astype(jnp.bfloat16), 'tp', scatter_dimensio...  18.9 us
    convert_element_type x2, local copies, waits for them, and re-layouts, body(): returned.reshape(E, 2, CAP, width).astype(jnp.float32)  17.8 us
  transfers between devices with their start and end apart: 3, of which 3 were waited for; matrix products, arithmetic and copies ran while one was open for 1% of the time, Pallas kernels for 0%

commit v1 on v0

--- a/solution.py
+++ b/solution.py
@@ -1,8 +1,11 @@
+import functools
 import math
 
 import jax
 import jax.numpy as jnp
 from jax import lax
+from jax.experimental import pallas as pl
+from jax.experimental.pallas import tpu as pltpu
 from jax.sharding import PartitionSpec as P
 
 HD = 128
@@ -21,7 +24,7 @@
     return (flatten, jnp.sum(earlier * chosen, axis=1))
 
 
-def body(
+def wide_body(
     hidden_in,
     queries,
     keys_new,
@@ -139,6 +142,458 @@
     return (state_cols + expert_cols).astype(jnp.bfloat16)
 
 
+EXT = 128
+MESH = pl.DeviceIdType.MESH
+
+
+def layer_kernel(
+    n_req,
+    n_tp,
+    req_group,
+    lengths,
+    hidden,
+    gain,
+    queries,
+    keys,
+    values,
+    prefix,
+    routes,
+    router,
+    w_out_hbm,
+    w_gate_hbm,
+    w_up_hbm,
+    w_down_hbm,
+    out,
+    w_out,
+    w_gate,
+    w_up,
+    w_down,
+    pre,
+    heads,
+    proj,
+    proj_in,
+    resid,
+    rows_all,
+    gates,
+    scale,
+    inner,
+    part,
+    core_in,
+    core_sum,
+    x_in,
+    x_sum,
+    y_in,
+    y_sum,
+    z_in,
+    load_sem,
+    pre_send,
+    pre_recv,
+    proj_send,
+    proj_recv,
+    gz_send,
+    gz_recv,
+    gy_send,
+    gy_recv,
+    gx_send,
+    gx_recv,
+    gc_send,
+    gc_recv,
+    rc_send,
+    rc_recv,
+    rx_send,
+    rx_recv,
+    ry_send,
+    ry_recv,
+    rz_send,
+    rz_recv,
+):
+    rows, cols = hidden.shape
+    n_z = n_req // 2
+    total = n_req * rows
+    req, tp = lax.axis_index("req"), lax.axis_index("tp")
+    z, y = req // 2, req % 2
+    x, core = tp // 2, tp % 2
+    y_peer = z * 2 + (1 - y)
+    x_peer = (1 - x) * 2 + core
+    c_peer = x * 2 + (1 - core)
+
+    loads = [
+        pltpu.make_async_copy(source, target, load_sem.at[i])
+        for i, (source, target) in enumerate(
+            [(w_out_hbm, w_out), (w_gate_hbm, w_gate), (w_up_hbm, w_up), (w_down_hbm, w_down)]
+        )
+    ]
+    for load in loads:
+        load.start()
+
+    barrier = pltpu.get_barrier_semaphore()
+    for k in range(1, n_req):
+        pl.semaphore_signal(
+            barrier, inc=1, device_id={"req": (req + k) % n_req}, device_id_type=MESH
+        )
+    for k in range(1, n_tp):
+        pl.semaphore_signal(barrier, inc=1, device_id={"tp": (tp + k) % n_tp}, device_id_type=MESH)
+    pl.semaphore_wait(barrier, n_req + n_tp - 2)
+
+    def send(source, target, send_sem, recv_sem, axis, peer):
+        copy = pltpu.make_async_remote_copy(
+            src_ref=source,
+            dst_ref=target,
+            send_sem=send_sem,
+            recv_sem=recv_sem,
+            device_id={axis: peer},
+            device_id_type=MESH,
+        )
+        copy.start()
+        return copy
+
+    copies = [
+        send(prefix, pre.at[k], pre_send.at[k], pre_recv.at[k], "req", (req + k) % n_req)
+        for k in range(1, n_req)
+    ]
+    pre[0] = prefix[...]
+    for copy in copies:
+        copy.wait()
+
+    blk = prefix.shape[0] // 2
+    n_pre = n_req * blk
+    ones = jnp.full((rows, EXT), 1.0 / EXT, jnp.bfloat16)
+    nt = (((1,), (1,)), ((), ()))
+    groups = pre[:, :blk, cols:].reshape(n_pre, EXT)
+    group_row = lax.dot_general(ones, groups, nt, preferred_element_type=jnp.float32)
+    pre_seen = group_row == req_group[0].astype(jnp.float32)
+    own_seen = lax.broadcasted_iota(jnp.int32, (rows, rows), 1) < lengths[0]
+    factor = 1.0 / math.sqrt(HD)
+    for h in range(cols // HD):
+        lanes = slice(h * HD, (h + 1) * HD)
+        q = queries[:, lanes]
+        pre_k = pre[:, :blk, lanes].reshape(n_pre, HD)
+        pre_v = pre[:, blk:, lanes].reshape(n_pre, HD)
+        s_pre = lax.dot_general(q, pre_k, nt, preferred_element_type=jnp.float32) * factor
+        s_own = (
+            lax.dot_general(q, keys[:, lanes], nt, preferred_element_type=jnp.float32) * factor
+        )
+        s_pre = jnp.where(pre_seen, s_pre, -jnp.inf)
+        s_own = jnp.where(own_seen, s_own, -jnp.inf)
+        top = jnp.maximum(
+            jnp.max(s_pre, axis=1, keepdims=True), jnp.max(s_own, axis=1, keepdims=True)
+        )
+        p_pre, p_own = jnp.exp(s_pre - top), jnp.exp(s_own - top)
+        denom = jnp.sum(p_pre, axis=1, keepdims=True) + jnp.sum(p_own, axis=1, keepdims=True)
+        mixed = jnp.dot(p_pre.astype(jnp.bfloat16), pre_v, preferred_element_type=jnp.float32)
+        mixed = mixed + jnp.dot(
+            p_own.astype(jnp.bfloat16), values[:, lanes], preferred_element_type=jnp.float32
+        )
+        heads[:, lanes] = (mixed / denom).astype(jnp.bfloat16)
+
+    loads[0].wait()
+    for t in range(n_tp):
+        proj[t] = jnp.dot(
+            heads[...], w_out[:, t * cols : (t + 1) * cols], preferred_element_type=jnp.float32
+        ).astype(jnp.bfloat16)
+    copies = []
+    for k in range(1, n_tp):
+        peer = (tp + k) % n_tp
+        copies.append(
+            send(proj.at[peer], proj_in.at[k], proj_send.at[k], proj_recv.at[k], "tp", peer)
+        )
+    chunk = hidden[...].astype(jnp.float32) + proj[tp].astype(jnp.float32)
+    for copy in copies:
+        copy.wait()
+    for k in range(1, n_tp):
+        chunk = chunk + proj_in[k].astype(jnp.float32)
+    resid[...] = chunk
+
+    lane = lax.broadcasted_iota(jnp.int32, (rows, EXT), 1)
+    square = jnp.sum(chunk * chunk, axis=1, keepdims=True)
+    high = square.astype(jnp.bfloat16).astype(jnp.float32)
+    middle = (square - high).astype(jnp.bfloat16).astype(jnp.float32)
+    low = square - high - middle
+    extra = jnp.where(lane == 0, high, jnp.where(lane == 1, middle, 0.0))
+    extra = jnp.where(lane == 2, low, extra)
+    for k in range(TOPK):
+        extra = jnp.where(lane == routes[:, k : k + 1] + (EXT - E), 1.0, extra)
+    rows_all[tp, 0, 0, :, :cols] = (chunk * gain[...].astype(jnp.float32)).astype(jnp.bfloat16)
+    rows_all[tp, 0, 0, :, cols:] = extra.astype(jnp.bfloat16)
+
+    own = rows_all.at[tp, 0, 0]
+    z_copies = [
+        send(
+            own,
+            rows_all.at[tp, 0, k],
+            gz_send.at[k],
+            gz_recv.at[k],
+            "req",
+            ((z + k) % n_z) * 2 + y,
+        )
+        for k in range(1, n_z)
+    ]
+    for copy in z_copies:
+        copy.wait()
+    near = rows_all.at[tp, 0]
+    far = rows_all.at[tp, 1]
+    y_copy = send(near, far, gy_send, gy_recv, "req", y_peer)
+    x_near = send(near, near, gx_send.at[0], gx_recv.at[0], "tp", x_peer)
+    c_near = send(near, near, gc_send.at[0], gc_recv.at[0], "tp", c_peer)
+    y_copy.wait()
+    x_far = send(far, far, gx_send.at[1], gx_recv.at[1], "tp", x_peer)
+    c_far = send(far, far, gc_send.at[1], gc_recv.at[1], "tp", c_peer)
+    x_near.wait()
+    over_near = rows_all.at[x_peer, 0]
+    d_near = send(over_near, over_near, gc_send.at[2], gc_recv.at[2], "tp", c_peer)
+    x_far.wait()
+    over_far = rows_all.at[x_peer, 1]
+    d_far = send(over_far, over_far, gc_send.at[3], gc_recv.at[3], "tp", c_peer)
+    c_near.wait()
+    c_far.wait()
+    d_near.wait()
+    d_far.wait()
+
+    lane_all = lax.broadcasted_iota(jnp.int32, (total, EXT), 1)
+    extras = jnp.zeros((total, EXT), jnp.float32)
+    logits = jnp.zeros((total, 3 * EXT), jnp.float32)
+    for t in range(n_tp):
+        extras = extras + rows_all[t, :, :, :, cols:].reshape(total, EXT).astype(jnp.float32)
+        logits = logits + jnp.dot(
+            rows_all[t, :, :, :, :cols].reshape(total, cols),
+            router[t * cols : (t + 1) * cols, :],
+            preferred_element_type=jnp.float32,
+        )
+    squares = jnp.sum(jnp.where(lane_all < 3, extras, 0.0), axis=1, keepdims=True)
+    factor_all = lax.rsqrt(squares / (n_tp * cols) + epsilon)
+    routed = (lane_all >= EXT - E) & (extras > 0.5)
+    logits = (logits[:, :EXT] + logits[:, EXT : 2 * EXT] + logits[:, 2 * EXT :]) * factor_all
+    logits = jnp.where(routed, logits, -jnp.inf)
+    powers = jnp.exp(logits - jnp.max(logits, axis=1, keepdims=True))
+    gates[...] = powers / jnp.sum(powers, axis=1, keepdims=True)
+    scale[...] = jnp.broadcast_to(factor_all, (total, EXT))
+
+    halves, depth, units = w_gate.shape
+    loads[1].wait()
+    loads[2].wait()
+
+    def half_step(j, carry):
+        both = jnp.zeros((total, 2 * units), jnp.float32)
+        for t in range(n_tp):
+            weights = jnp.concatenate(
+                [w_gate[j, t * cols : (t + 1) * cols, :], w_up[j, t * cols : (t + 1) * cols, :]],
+                axis=1,
+            )
+            both = both + jnp.dot(
+                rows_all[t, :, :, :, :cols].reshape(total, cols),
+                weights,
+                preferred_element_type=jnp.float32,
+            )
+        expert = (req * halves + j) // 2 + (EXT - E)
+        gate_col = jnp.sum(
+            jnp.where(lane_all == expert, gates[...], 0.0), axis=1, keepdims=True
+        )
+        gate_val = both[:, :units] * scale[:, :units]
+        up_val = both[:, units:] * scale[:, :units]
+        value = gate_val / (1.0 + jnp.exp(-gate_val)) * up_val * gate_col
+        inner[:, pl.ds(pl.multiple_of(j * units, units), units)] = value.astype(jnp.bfloat16)
+        return carry
+
+    lax.fori_loop(0, halves, half_step, 0)
+    loads[3].wait()
+
+    def down(t):
+        where = pl.ds(pl.multiple_of(t * cols, cols), cols)
+        result = jnp.dot(
+            inner[...],
+            w_down[:, :, where].reshape(halves * units, cols),
+            preferred_element_type=jnp.float32,
+        )
+        part[t] = result.astype(jnp.bfloat16).reshape(2, n_z, rows, cols)
+
+    def plus(first, second):
+        return (first.astype(jnp.float32) + second.astype(jnp.float32)).astype(jnp.bfloat16)
+
+    down((1 - x) * 2 + (1 - core))
+    over = send(
+        part.at[(1 - x) * 2 + (1 - core)],
+        core_in.at[0],
+        rc_send.at[0],
+        rc_recv.at[0],
+        "tp",
+        c_peer,
+    )
+    down((1 - x) * 2 + core)
+    over.wait()
+    x_copies = []
+    for side in (1, 0):
+        core_sum[0, side] = plus(part[(1 - x) * 2 + core, side], core_in[0, side])
+        x_copies.append(
+            send(
+                core_sum.at[0, side],
+                x_in.at[side],
+                rx_send.at[side],
+                rx_recv.at[side],
+                "tp",
+                x_peer,
+            )
+        )
+    down(x * 2 + (1 - core))
+    here = send(
+        part.at[x * 2 + (1 - core)],
+        core_in.at[1],
+        rc_send.at[1],
+        rc_recv.at[1],
+        "tp",
+        c_peer,
+    )
+    down(x * 2 + core)
+    here.wait()
+    x_copies[0].wait()
+    x_sum[1] = (
+        part[x * 2 + core, 1].astype(jnp.float32)
+        + core_in[1, 1].astype(jnp.float32)
+        + x_in[1].astype(jnp.float32)
+    ).astype(jnp.bfloat16)
+    y_copy = send(x_sum.at[1], y_in, ry_send, ry_recv, "req", y_peer)
+    x_copies[1].wait()
+    near_sum = (
+        part[x * 2 + core, 0].astype(jnp.float32)
+        + core_in[1, 0].astype(jnp.float32)
+        + x_in[0].astype(jnp.float32)
+    )
+    y_copy.wait()
+    near_sum = near_sum + y_in[...].astype(jnp.float32)
+    y_sum[...] = near_sum.astype(jnp.bfloat16)
+    z_copies = [
+        send(
+            y_sum.at[k],
+            z_in.at[k],
+            rz_send.at[k],
+            rz_recv.at[k],
+            "req",
+            ((z + n_z - k) % n_z) * 2 + y,
+        )
+        for k in range(1, n_z)
+    ]
+    result = resid[...] + near_sum[0]
+    for copy in z_copies:
+        copy.wait()
+    for k in range(1, n_z):
+        result = result + z_in[k].astype(jnp.float32)
+    out[...] = result.astype(jnp.bfloat16)
+
+
+def split_router(w_router):
+    rest, pieces = w_router, []
+    for _ in range(3):
+        piece = lax.reduce_precision(rest, 8, 7)
+        pieces.append(jnp.pad(piece, ((0, 0), (EXT - E, 0))).astype(jnp.bfloat16))
+        rest = rest - piece
+    return jnp.concatenate(pieces, axis=1)
+
+
+def body(
+    hidden_in,
+    queries,
+    keys_new,
+    values_new,
+    prefix_keys,
+    prefix_values,
+    block_group,
+    req_group,
+    lengths,
+    w_out,
+    norm_gain,
+    w_router,
+    routes,
+    w_gate,
+    w_up,
+    w_down,
+):
+    n_req, n_tp = lax.axis_size("req"), lax.axis_size("tp")
+    rows, width = hidden_in.shape
+    cols = width // n_tp
+    blk = prefix_keys.shape[1]
+    start = lax.axis_index("tp") * cols
+    hidden = lax.dynamic_slice_in_dim(hidden_in, start, cols, 1)
+    gain = lax.dynamic_slice_in_dim(norm_gain, start, cols, 0).reshape(1, cols)
+    both = jnp.concatenate([prefix_keys[0], prefix_values[0]], axis=0)
+    group = jnp.broadcast_to(block_group.astype(jnp.bfloat16)[:, None], (2 * blk, EXT))
+    prefix = jnp.concatenate([both, group], axis=1)
+    n_z = n_req // 2
+    total = n_req * rows
+    halves, _, units = w_gate.shape
+    bf16, f32 = jnp.bfloat16, jnp.float32
+    dma = pltpu.SemaphoreType.DMA
+    vmem = pl.BlockSpec(memory_space=pltpu.VMEM)
+    smem = pl.BlockSpec(memory_space=pltpu.SMEM)
+    hbm = pl.BlockSpec(memory_space=pl.ANY)
+    return pl.pallas_call(
+        functools.partial(layer_kernel, n_req, n_tp),
+        out_shape=jax.ShapeDtypeStruct((rows, cols), bf16),
+        in_specs=[smem] * 2 + [vmem] * 8 + [hbm] * 4,
+        out_specs=vmem,
+        scratch_shapes=[
+            pltpu.VMEM(w_out.shape, bf16),
+            pltpu.VMEM(w_gate.shape, bf16),
+            pltpu.VMEM(w_up.shape, bf16),
+            pltpu.VMEM(w_down.shape, bf16),
+            pltpu.VMEM((n_req, 2 * blk, cols + EXT), bf16),
+            pltpu.VMEM((rows, cols), bf16),
+            pltpu.VMEM((n_tp, rows, cols), bf16),
+            pltpu.VMEM((n_tp, rows, cols), bf16),
+            pltpu.VMEM((rows, cols), f32),
+            pltpu.VMEM((n_tp, 2, n_z, rows, cols + EXT), bf16),
+            pltpu.VMEM((total, EXT), f32),
+            pltpu.VMEM((total, EXT), f32),
+            pltpu.VMEM((total, halves * units), bf16),
+            pltpu.VMEM((n_tp, 2, n_z, rows, cols), bf16),
+            pltpu.VMEM((2, 2, n_z, rows, cols), bf16),
+            pltpu.VMEM((1, 2, n_z, rows, cols), bf16),
+            pltpu.VMEM((2, n_z, rows, cols), bf16),
+            pltpu.VMEM((2, n_z, rows, cols), bf16),
+            pltpu.VMEM((n_z, rows, cols), bf16),
+            pltpu.VMEM((n_z, rows, cols), bf16),
+            pltpu.VMEM((n_z, rows, cols), bf16),
+            dma((4,)),
+            dma((n_req,)),
+            dma((n_req,)),
+            dma((n_tp,)),
+            dma((n_tp,)),
+            dma((n_z,)),
+            dma((n_z,)),
+            dma,
+            dma,
+            dma((2,)),
+            dma((2,)),
+            dma((4,)),
+            dma((4,)),
+            dma((2,)),
+            dma((2,)),
+            dma((2,)),
+            dma((2,)),
+            dma,
+            dma,
+            dma((n_z,)),
+            dma((n_z,)),
+        ],
+        compiler_params=pltpu.CompilerParams(
+            collective_id=0, has_side_effects=True, vmem_limit_bytes=56 * 1024 * 1024
+        ),
+    )(
+        req_group,
+        lengths,
+        hidden,
+        gain,
+        queries,
+        keys_new,
+        values_new,
+        prefix,
+        routes,
+        split_router(w_router),
+        w_out,
+        w_gate,
+        w_up,
+        w_down,
+    )
+
+
 def solution(mesh):
     in_specs = (
         P("req", None),
@@ -159,4 +614,6 @@
         P("req", "tp", None),
     )
     out_specs = P("req", "tp")
-    return jax.shard_map(body, mesh=mesh, in_specs=in_specs, out_specs=out_specs, check_vma=False)
+    n_req, n_tp = mesh.shape["req"], mesh.shape["tp"]
+    fits = n_req <= 8 and n_req % 2 == 0 and n_tp == 4
+    return jax.shard_map(body if fits else wide_body, mesh=mesh, in_specs=in_specs, out_specs=out_specs, check_vma=False)

time: 588 us -> 101 us (0.17)
  blocking collectives: 272 us -> 0 us
  waiting for transfers between devices: 159 us -> 0 us
  Pallas kernels: 0 us -> 87.8 us
  local copies, waits for them, and re-layouts: 63 us -> 6.82 us
  matrix products: 42 us -> 0 us
  other arithmetic: 26.5 us -> 3.7 us
  between operations: 16.2 us -> 2.04 us
    all_to_all x1 -> x0, blocking collectives: 187 us -> none  [body(): lax.all_to_all(doubled, 'req', split_axis=0, concat_axis=1, tiled=True)]
    all_to_all x1 -> x0, waiting for transfers between devices: 113 us -> none  [body(): lax.all_to_all(pieces, 'req', split_axis=1, concat_axis=0, tiled=True)]
    pallas_call x0 -> x1, Pallas kernels: none -> 87.8 us  [body(): pl.pallas_call(functools.partial(layer_kernel, n_req, n_tp), out_shape=ja...]
    all_gather x2 -> x0, blocking collectives: 61.5 us -> none  [the longest x1 30.7 us: body(): piece_values = lax.all_gather(prefix_values, 'req', axis=0, tiled=True)]
    dot_general x10 -> x0, matrix products: 42 us -> none  [the longest x1 17.3 us: body(): jnp.einsum('lrf,lfd->lrd', inner, w_down, preferred_element_type=jnp.floa...]
    psum x1 -> x0, waiting for transfers between devices: 26.7 us -> none  [body(): lax.psum(partial_value.astype(jnp.bfloat16), 'tp').astype(jnp.float32)]
    convert_element_type x3 -> x0, local copies, waits for them, and re-layouts: 25.5 us -> none  [the longest x2 17.8 us: body(): returned.reshape(E, 2, CAP, width).astype(jnp.float32)]
    unnamed x1 -> x0, blocking collectives: 23.1 us -> none
  transfers between devices with their start and end apart: 3 -> 0, of which waited for: 3 -> 0; matrix products, arithmetic and copies ran while one was open for 1% -> 0% of each run, Pallas kernels for 0% -> 0%
where the time goes in v1:
time: 101 us; the launch traced here: 100 us
  Pallas kernels  87.8 us (87%)
  local copies, waits for them, and re-layouts  6.82 us (7%)
  other arithmetic  3.7 us (4%)
  between operations  2.04 us (2%)
    pallas_call x1, Pallas kernels, body(): pl.pallas_call(functools.partial(layer_kernel, n_req, n_tp), out_shape=ja...  87.8 us
    unnamed x11, local copies, waits for them, and re-layouts  4.5 us

profile of v1, /device:TPU:0, one launch (start us, length us, event | category | flops | bytes accessed | tf_op | source)
XLA Modules:
  0.0 100.4 jit_solution(152670350116697056)
XLA Ops:
  0.0 0.0 copy-start
  0.0 0.9 copy-done
  1.0 0.6 constant_dynamic-slice_fusion.hidden
  1.6 0.8 dynamic_slice.7
  2.3 0.6 reshape.4.gain
  2.9 1.1 %reduce_precision.9 = f32[2048,64]{0,1:T(8,128)S(1)} reduce-precision(f32[2048,64]{0,1:T(8,128)} %param.27), exponent_bits=8, mantissa_bits=7 | non-fusion elementwise | flops 131072 | bytes 1048576 | tf_op jit(solution)/shard_map/reduce_precision | solution.py:485
  4.0 0.3 copy.20
  4.4 1.4 %copy.21 = f32[2048,64]{1,0:T(8,128)S(1)} copy(f32[2048,64]{0,1:T(8,128)} %param.27) | data formatting | bytes 1048576 | tf_op args[11]
  5.7 0.0 copy-start.1
  5.8 0.0 copy-start.2
  5.8 0.0 copy-start.3
  5.8 0.2 reduce-precision_convert_fusion
  6.0 1.8 %fusion.5.router = bf16[2048,384]{1,0:T(8,128)(2,1)} fusion(bf16[2048,64]{1,0:T(8,128)(2,1)S(1)} %get-tuple-element.6, bf16[2048,64]{1,0:T(8,128)(2,1)S(1)} %get-tuple-element.5, bf16[2048,64]{1,0:T(8,128)(2,1)S(1)} %get-tuple-element.7), kind=kLoop, calls=%fused_computation.9 | loop fusion | flops 11010048 | bytes 2359296 | tf_op jit(solution)/shard_map/concatenate | solution.py:488
  8.4 0.0 copy-done.1
  8.5 0.0 copy-done.2
  8.5 0.6 fusion.10.prefix
  9.1 0.0 copy-done.3
  9.1 0.7 copy.23.routes
  11.1 87.8 %shard_map.154 = bf16[64,512]{1,0:T(8,128)(2,1)} custom-call(s32[1]{0:T(128)S(6)} %copy.26.req_group, s32[1]{0:T(128)S(6)} %copy.27.lengths, bf16[64,512]{1,0:T(8,128)(2,1)} %constant_dynamic-slice_fusion.hidden, bf16[1,512]{1,0:T(2,128)(2,1)} %reshape.4.gain, bf16[64,512]{1,0:T(8,128)(2,1)} %queries.1, bf16[64,512]{1,0:T(8,128)(2,1)} %keys.1, ...), custom_call_target="tpu_custom_call" | custom-call | tf_op jit(solution)/shard_map/pallas_call | solution.py:527
  98.9 1.5 %copy.28 = bf16[64,512]{1,0:T(8,128)(2,1)} copy(bf16[64,512]{1,0:T(8,128)(2,1)} %shard_map.154) | data formatting | bytes 131072
Async XLA Ops:
  0.0 1.0 copy-start
  5.7 2.7 %copy-start.1 = (bf16[1,16,512]{2,1,0:T(8,128)(2,1)S(1)}, bf16[1,16,512]{2,1,0:T(8,128)(2,1)}, u32[]{:S(2)}) copy-start(bf16[1,16,512]{2,1,0:T(8,128)(2,1)} %param.21) | copy-start | bytes 49156
  5.8 2.7 %copy-start.2 = (bf16[1,16,512]{2,1,0:T(8,128)(2,1)S(1)}, bf16[1,16,512]{2,1,0:T(8,128)(2,1)}, u32[]{:S(2)}) copy-start(bf16[1,16,512]{2,1,0:T(8,128)(2,1)} %param.20) | copy-start | bytes 49156
  5.8 3.3 %copy-start.3 = (s32[64,8]{0,1:T(8,128)S(1)}, s32[64,8]{0,1:T(8,128)}, u32[]{:S(2)}) copy-start(s32[64,8]{0,1:T(8,128)} %param.28) | copy-start | bytes 6148

commit v2 on v1

--- a/solution.py
+++ b/solution.py
@@ -151,14 +151,16 @@
     n_tp,
     req_group,
     lengths,
+    block_group,
     hidden,
     gain,
     queries,
     keys,
     values,
-    prefix,
+    prefix_keys,
+    prefix_values,
     routes,
-    router,
+    w_router,
     w_out_hbm,
     w_gate_hbm,
     w_up_hbm,
@@ -168,6 +170,7 @@
     w_gate,
     w_up,
     w_down,
+    router,
     pre,
     heads,
     proj,
@@ -207,9 +210,11 @@
     rz_send,
     rz_recv,
 ):
-    rows, cols = hidden.shape
+    rows, cols = queries.shape
+    blk = prefix_keys.shape[1]
     n_z = n_req // 2
-    total = n_req * rows
+    total = n_z * rows
+    order = sorted(range(n_z), key=lambda k: min(k, n_z - k))
     req, tp = lax.axis_index("req"), lax.axis_index("tp")
     z, y = req // 2, req % 2
     x, core = tp // 2, tp % 2
@@ -225,6 +230,12 @@
     ]
     for load in loads:
         load.start()
+
+    pre[0, :blk, :cols] = prefix_keys[0]
+    pre[0, blk:, :cols] = prefix_values[0]
+    pre[0, :, cols:] = jnp.full((2 * blk, EXT), block_group[0].astype(jnp.float32)).astype(
+        jnp.bfloat16
+    )
 
     barrier = pltpu.get_barrier_semaphore()
     for k in range(1, n_req):
@@ -248,14 +259,18 @@
         return copy
 
     copies = [
-        send(prefix, pre.at[k], pre_send.at[k], pre_recv.at[k], "req", (req + k) % n_req)
+        send(pre.at[0], pre.at[k], pre_send.at[k], pre_recv.at[k], "req", (req + k) % n_req)
         for k in range(1, n_req)
     ]
-    pre[0] = prefix[...]
+    rest = w_router[...]
+    for i in range(3):
+        piece = rest.astype(jnp.bfloat16)
+        router[i * EXT : i * EXT + EXT - E, :] = jnp.zeros_like(piece)
+        router[i * EXT + EXT - E : (i + 1) * EXT, :] = piece
+        rest = rest - piece.astype(jnp.float32)
     for copy in copies:
         copy.wait()
 
-    blk = prefix.shape[0] // 2
     n_pre = n_req * blk
     ones = jnp.full((rows, EXT), 1.0 / EXT, jnp.bfloat16)
     nt = (((1,), (1,)), ((), ()))
@@ -297,7 +312,8 @@
         copies.append(
             send(proj.at[peer], proj_in.at[k], proj_send.at[k], proj_recv.at[k], "tp", peer)
         )
-    chunk = hidden[...].astype(jnp.float32) + proj[tp].astype(jnp.float32)
+    own_cols = pl.ds(pl.multiple_of(tp * cols, cols), cols)
+    chunk = hidden[:, own_cols].astype(jnp.float32) + proj[tp].astype(jnp.float32)
     for copy in copies:
         copy.wait()
     for k in range(1, n_tp):
@@ -311,9 +327,17 @@
     low = square - high - middle
     extra = jnp.where(lane == 0, high, jnp.where(lane == 1, middle, 0.0))
     extra = jnp.where(lane == 2, low, extra)
+    experts = lax.broadcasted_iota(jnp.int32, (EXT, rows), 0) - (EXT - E)
+    named = jnp.zeros((EXT, rows), jnp.float32)
     for k in range(TOPK):
-        extra = jnp.where(lane == routes[:, k : k + 1] + (EXT - E), 1.0, extra)
-    rows_all[tp, 0, 0, :, :cols] = (chunk * gain[...].astype(jnp.float32)).astype(jnp.bfloat16)
+        named = jnp.where(experts == routes[k : k + 1, :], 1.0, named)
+    first = lax.broadcasted_iota(jnp.int32, (rows, rows), 0)
+    second = lax.broadcasted_iota(jnp.int32, (rows, rows), 1)
+    eye = jnp.where(first == second, 1.0, 0.0).astype(jnp.bfloat16)
+    extra = extra + lax.dot_general(
+        eye, named.astype(jnp.bfloat16), nt, preferred_element_type=jnp.float32
+    )
+    rows_all[tp, 0, 0, :, :cols] = (chunk * gain[:, own_cols].astype(jnp.float32)).astype(jnp.bfloat16)
     rows_all[tp, 0, 0, :, cols:] = extra.astype(jnp.bfloat16)
 
     own = rows_all.at[tp, 0, 0]
@@ -328,164 +352,186 @@
         )
         for k in range(1, n_z)
     ]
-    for copy in z_copies:
-        copy.wait()
-    near = rows_all.at[tp, 0]
-    far = rows_all.at[tp, 1]
-    y_copy = send(near, far, gy_send, gy_recv, "req", y_peer)
-    x_near = send(near, near, gx_send.at[0], gx_recv.at[0], "tp", x_peer)
-    c_near = send(near, near, gc_send.at[0], gc_recv.at[0], "tp", c_peer)
-    y_copy.wait()
-    x_far = send(far, far, gx_send.at[1], gx_recv.at[1], "tp", x_peer)
-    c_far = send(far, far, gc_send.at[1], gc_recv.at[1], "tp", c_peer)
-    x_near.wait()
-    over_near = rows_all.at[x_peer, 0]
-    d_near = send(over_near, over_near, gc_send.at[2], gc_recv.at[2], "tp", c_peer)
-    x_far.wait()
-    over_far = rows_all.at[x_peer, 1]
-    d_far = send(over_far, over_far, gc_send.at[3], gc_recv.at[3], "tp", c_peer)
-    c_near.wait()
-    c_far.wait()
-    d_near.wait()
-    d_far.wait()
-
+    arrived = {k: copy for k, copy in zip(range(1, n_z), z_copies)}
+    y_copies, x_near, c_near, x_far, c_far, d_near, d_far = {}, {}, {}, {}, {}, {}, {}
+
+    def over_x(side, k):
+        block = rows_all.at[tp, side, k]
+        return send(block, block, gx_send.at[side, k], gx_recv.at[side, k], "tp", x_peer)
+
+    def over_core(owner, i, side, k):
+        block = rows_all.at[owner, side, k]
+        return send(block, block, gc_send.at[i, side, k], gc_recv.at[i, side, k], "tp", c_peer)
+
+    for k in order:
+        if k > 0:
+            arrived[k].wait()
+        x_near[k] = over_x(0, k)
+        y_copies[k] = send(
+            rows_all.at[tp, 0, k],
+            rows_all.at[tp, 1, k],
+            gy_send.at[k],
+            gy_recv.at[k],
+            "req",
+            y_peer,
+        )
+        c_near[k] = over_core(tp, 0, 0, k)
+    for k in order:
+        x_near[k].wait()
+        d_near[k] = over_core(x_peer, 1, 0, k)
+    for k in order:
+        y_copies[k].wait()
+        x_far[k] = over_x(1, k)
+        c_far[k] = over_core(tp, 0, 1, k)
+    for k in order:
+        c_near[k].wait()
+        d_near[k].wait()
+
+    halves, depth, units = w_gate.shape
     lane_all = lax.broadcasted_iota(jnp.int32, (total, EXT), 1)
-    extras = jnp.zeros((total, EXT), jnp.float32)
-    logits = jnp.zeros((total, 3 * EXT), jnp.float32)
-    for t in range(n_tp):
-        extras = extras + rows_all[t, :, :, :, cols:].reshape(total, EXT).astype(jnp.float32)
-        logits = logits + jnp.dot(
-            rows_all[t, :, :, :, :cols].reshape(total, cols),
-            router[t * cols : (t + 1) * cols, :],
-            preferred_element_type=jnp.float32,
-        )
-    squares = jnp.sum(jnp.where(lane_all < 3, extras, 0.0), axis=1, keepdims=True)
-    factor_all = lax.rsqrt(squares / (n_tp * cols) + epsilon)
-    routed = (lane_all >= EXT - E) & (extras > 0.5)
-    logits = (logits[:, :EXT] + logits[:, EXT : 2 * EXT] + logits[:, 2 * EXT :]) * factor_all
-    logits = jnp.where(routed, logits, -jnp.inf)
-    powers = jnp.exp(logits - jnp.max(logits, axis=1, keepdims=True))
-    gates[...] = powers / jnp.sum(powers, axis=1, keepdims=True)
-    scale[...] = jnp.broadcast_to(factor_all, (total, EXT))
-
-    halves, depth, units = w_gate.shape
-    loads[1].wait()
-    loads[2].wait()
-
-    def half_step(j, carry):
-        both = jnp.zeros((total, 2 * units), jnp.float32)
+
+    def rows_of(side):
+        return jnp.concatenate(
+            [rows_all[t, side, :, :, :cols].reshape(total, cols) for t in range(n_tp)], axis=1
+        )
+
+    def find_gates(side):
+        extras = jnp.zeros((total, EXT), jnp.float32)
         for t in range(n_tp):
-            weights = jnp.concatenate(
-                [w_gate[j, t * cols : (t + 1) * cols, :], w_up[j, t * cols : (t + 1) * cols, :]],
-                axis=1,
+            extras = extras + rows_all[t, side, :, :, cols:].reshape(total, EXT).astype(jnp.float32)
+        logits = lax.dot_general(
+            rows_of(side), router[...], nt, preferred_element_type=jnp.float32
+        )
+        squares = jnp.sum(jnp.where(lane_all < 3, extras, 0.0), axis=1, keepdims=True)
+        factor_all = lax.rsqrt(squares / (n_tp * cols) + epsilon)
+        routed = (lane_all >= EXT - E) & (extras > 0.5)
+        logits = (logits[:, :EXT] + logits[:, EXT : 2 * EXT] + logits[:, 2 * EXT :]) * factor_all
+        logits = jnp.where(routed, logits, -jnp.inf)
+        powers = jnp.exp(logits - jnp.max(logits, axis=1, keepdims=True))
+        gates[...] = powers / jnp.sum(powers, axis=1, keepdims=True)
+        scale[...] = jnp.broadcast_to(factor_all, (total, EXT))
+
+    def hidden_units(side, begin, end):
+        def half_step(j, carry):
+            weights = jnp.concatenate([w_gate[j], w_up[j]], axis=1)
+            both = jnp.dot(rows_of(side), weights, preferred_element_type=jnp.float32)
+            expert = (req * halves + j) // 2 + (EXT - E)
+            gate_col = jnp.sum(
+                jnp.where(lane_all == expert, gates[...], 0.0), axis=1, keepdims=True
             )
-            both = both + jnp.dot(
-                rows_all[t, :, :, :, :cols].reshape(total, cols),
-                weights,
-                preferred_element_type=jnp.float32,
-            )
-        expert = (req * halves + j) // 2 + (EXT - E)
-        gate_col = jnp.sum(
-            jnp.where(lane_all == expert, gates[...], 0.0), axis=1, keepdims=True
-        )
-        gate_val = both[:, :units] * scale[:, :units]
-        up_val = both[:, units:] * scale[:, :units]
-        value = gate_val / (1.0 + jnp.exp(-gate_val)) * up_val * gate_col
-        inner[:, pl.ds(pl.multiple_of(j * units, units), units)] = value.astype(jnp.bfloat16)
-        return carry
-
-    lax.fori_loop(0, halves, half_step, 0)
-    loads[3].wait()
-
-    def down(t):
+            gate_val = both[:, :units] * scale[:, :units]
+            up_val = both[:, units:] * scale[:, :units]
+            value = gate_val / (1.0 + jnp.exp(-gate_val)) * up_val * gate_col
+            inner[:, pl.ds(pl.multiple_of(j * units, units), units)] = value.astype(jnp.bfloat16)
+            return carry
+
+        lax.fori_loop(begin, end, half_step, 0, unroll=2)
+
+    def down(side, t):
         where = pl.ds(pl.multiple_of(t * cols, cols), cols)
         result = jnp.dot(
             inner[...],
             w_down[:, :, where].reshape(halves * units, cols),
             preferred_element_type=jnp.float32,
         )
-        part[t] = result.astype(jnp.bfloat16).reshape(2, n_z, rows, cols)
-
-    def plus(first, second):
-        return (first.astype(jnp.float32) + second.astype(jnp.float32)).astype(jnp.bfloat16)
-
-    down((1 - x) * 2 + (1 - core))
-    over = send(
-        part.at[(1 - x) * 2 + (1 - core)],
-        core_in.at[0],
-        rc_send.at[0],
-        rc_recv.at[0],
-        "tp",
-        c_peer,
-    )
-    down((1 - x) * 2 + core)
+        part[t, side] = result.astype(jnp.bfloat16).reshape(n_z, rows, cols)
+
+    def to_core(i, side, t):
+        return send(
+            part.at[t, side],
+            core_in.at[i, side],
+            rc_send.at[i, side],
+            rc_recv.at[i, side],
+            "tp",
+            c_peer,
+        )
+
+    def to_x(side, k):
+        mine = part[x_peer, side, k].astype(jnp.float32)
+        core_sum[side, k] = (mine + core_in[0, side, k].astype(jnp.float32)).astype(jnp.bfloat16)
+        return send(
+            core_sum.at[side, k],
+            x_in.at[side, k],
+            rx_send.at[side, k],
+            rx_recv.at[side, k],
+            "tp",
+            x_peer,
+        )
+
+    def three(side, k):
+        return (
+            part[tp, side, k].astype(jnp.float32)
+            + core_in[1, side, k].astype(jnp.float32)
+            + x_in[side, k].astype(jnp.float32)
+        )
+
+    over_t, here_t = (1 - x) * 2 + (1 - core), c_peer
+    last = halves - halves // 4
+    early = halves // 4
+
+    find_gates(0)
+    loads[1].wait()
+    loads[2].wait()
+    hidden_units(0, 0, last)
+    for k in order:
+        x_far[k].wait()
+        d_far[k] = over_core(x_peer, 1, 1, k)
+    hidden_units(0, last, halves)
+    loads[3].wait()
+    down(0, over_t)
+    over = to_core(0, 0, over_t)
+    down(0, here_t)
+    here = to_core(1, 0, here_t)
+    down(0, x_peer)
+    down(0, tp)
+
+    for k in order:
+        c_far[k].wait()
+        d_far[k].wait()
+    find_gates(1)
+    hidden_units(1, 0, early)
     over.wait()
-    x_copies = []
-    for side in (1, 0):
-        core_sum[0, side] = plus(part[(1 - x) * 2 + core, side], core_in[0, side])
-        x_copies.append(
-            send(
-                core_sum.at[0, side],
-                x_in.at[side],
-                rx_send.at[side],
-                rx_recv.at[side],
-                "tp",
-                x_peer,
+    here.wait()
+    x_first = [to_x(0, k) for k in range(n_z)]
+    hidden_units(1, early, halves)
+    down(1, over_t)
+    over = to_core(0, 1, over_t)
+    down(1, x_peer)
+    over.wait()
+    back = order[::-1]
+    x_second = {k: to_x(1, k) for k in back}
+    down(1, here_t)
+    here = to_core(1, 1, here_t)
+    down(1, tp)
+    here.wait()
+    for copy in x_first:
+        copy.wait()
+    y_back, z_back = {}, {}
+    for k in back:
+        x_second[k].wait()
+        x_sum[k] = three(1, k).astype(jnp.bfloat16)
+        y_back[k] = send(x_sum.at[k], y_in.at[k], ry_send.at[k], ry_recv.at[k], "req", y_peer)
+    for k in back:
+        near_sum = three(0, k)
+        y_back[k].wait()
+        near_sum = near_sum + y_in[k].astype(jnp.float32)
+        if k == 0:
+            resid[...] = resid[...] + near_sum
+        else:
+            y_sum[k] = near_sum.astype(jnp.bfloat16)
+            z_back[k] = send(
+                y_sum.at[k],
+                z_in.at[k],
+                rz_send.at[k],
+                rz_recv.at[k],
+                "req",
+                ((z + n_z - k) % n_z) * 2 + y,
             )
-        )
-    down(x * 2 + (1 - core))
-    here = send(
-        part.at[x * 2 + (1 - core)],
-        core_in.at[1],
-        rc_send.at[1],
-        rc_recv.at[1],
-        "tp",
-        c_peer,
-    )
-    down(x * 2 + core)
-    here.wait()
-    x_copies[0].wait()
-    x_sum[1] = (
-        part[x * 2 + core, 1].astype(jnp.float32)
-        + core_in[1, 1].astype(jnp.float32)
-        + x_in[1].astype(jnp.float32)
-    ).astype(jnp.bfloat16)
-    y_copy = send(x_sum.at[1], y_in, ry_send, ry_recv, "req", y_peer)
-    x_copies[1].wait()
-    near_sum = (
-        part[x * 2 + core, 0].astype(jnp.float32)
-        + core_in[1, 0].astype(jnp.float32)
-        + x_in[0].astype(jnp.float32)
-    )
-    y_copy.wait()
-    near_sum = near_sum + y_in[...].astype(jnp.float32)
-    y_sum[...] = near_sum.astype(jnp.bfloat16)
-    z_copies = [
-        send(
-            y_sum.at[k],
-            z_in.at[k],
-            rz_send.at[k],
-            rz_recv.at[k],
-            "req",
-            ((z + n_z - k) % n_z) * 2 + y,
-        )
-        for k in range(1, n_z)
-    ]
-    result = resid[...] + near_sum[0]
-    for copy in z_copies:
-        copy.wait()
+    result = resid[...]
     for k in range(1, n_z):
+        z_back[k].wait()
         result = result + z_in[k].astype(jnp.float32)
     out[...] = result.astype(jnp.bfloat16)
-
-
-def split_router(w_router):
-    rest, pieces = w_router, []
-    for _ in range(3):
-        piece = lax.reduce_precision(rest, 8, 7)
-        pieces.append(jnp.pad(piece, ((0, 0), (EXT - E, 0))).astype(jnp.bfloat16))
-        rest = rest - piece
-    return jnp.concatenate(pieces, axis=1)
 
 
 def body(
@@ -510,14 +556,8 @@
     rows, width = hidden_in.shape
     cols = width // n_tp
     blk = prefix_keys.shape[1]
-    start = lax.axis_index("tp") * cols
-    hidden = lax.dynamic_slice_in_dim(hidden_in, start, cols, 1)
-    gain = lax.dynamic_slice_in_dim(norm_gain, start, cols, 0).reshape(1, cols)
-    both = jnp.concatenate([prefix_keys[0], prefix_values[0]], axis=0)
-    group = jnp.broadcast_to(block_group.astype(jnp.bfloat16)[:, None], (2 * blk, EXT))
-    prefix = jnp.concatenate([both, group], axis=1)
     n_z = n_req // 2
-    total = n_req * rows
+    total = n_z * rows
     halves, _, units = w_gate.shape
     bf16, f32 = jnp.bfloat16, jnp.float32
     dma = pltpu.SemaphoreType.DMA
@@ -527,13 +567,14 @@
     return pl.pallas_call(
         functools.partial(layer_kernel, n_req, n_tp),
         out_shape=jax.ShapeDtypeStruct((rows, cols), bf16),
-        in_specs=[smem] * 2 + [vmem] * 8 + [hbm] * 4,
+        in_specs=[smem] * 3 + [vmem] * 9 + [hbm] * 4,
         out_specs=vmem,
         scratch_shapes=[
             pltpu.VMEM(w_out.shape, bf16),
             pltpu.VMEM(w_gate.shape, bf16),
             pltpu.VMEM(w_up.shape, bf16),
             pltpu.VMEM(w_down.shape, bf16),
+            pltpu.VMEM((3 * EXT, width), bf16),
             pltpu.VMEM((n_req, 2 * blk, cols + EXT), bf16),
             pltpu.VMEM((rows, cols), bf16),
             pltpu.VMEM((n_tp, rows, cols), bf16),
@@ -545,9 +586,9 @@
             pltpu.VMEM((total, halves * units), bf16),
             pltpu.VMEM((n_tp, 2, n_z, rows, cols), bf16),
             pltpu.VMEM((2, 2, n_z, rows, cols), bf16),
-            pltpu.VMEM((1, 2, n_z, rows, cols), bf16),
             pltpu.VMEM((2, n_z, rows, cols), bf16),
             pltpu.VMEM((2, n_z, rows, cols), bf16),
+            pltpu.VMEM((n_z, rows, cols), bf16),
             pltpu.VMEM((n_z, rows, cols), bf16),
             pltpu.VMEM((n_z, rows, cols), bf16),
             pltpu.VMEM((n_z, rows, cols), bf16),
@@ -558,18 +599,18 @@
             dma((n_tp,)),
             dma((n_z,)),
             dma((n_z,)),
-            dma,
-            dma,
-            dma((2,)),
-            dma((2,)),
-            dma((4,)),
-            dma((4,)),
-            dma((2,)),
-            dma((2,)),
-            dma((2,)),
-            dma((2,)),
-            dma,
-            dma,
+            dma((n_z,)),
+            dma((n_z,)),
+            dma((2, n_z)),
+            dma((2, n_z)),
+            dma((2, 2, n_z)),
+            dma((2, 2, n_z)),
+            dma((2, 2)),
+            dma((2, 2)),
+            dma((2, n_z)),
+            dma((2, n_z)),
+            dma((n_z,)),
+            dma((n_z,)),
             dma((n_z,)),
             dma((n_z,)),
         ],
@@ -579,14 +620,16 @@
     )(
         req_group,
         lengths,
-        hidden,
-        gain,
+        block_group,
+        hidden_in,
+        norm_gain.reshape(1, width),
         queries,
         keys_new,
         values_new,
-        prefix,
-        routes,
-        split_router(w_router),
+        prefix_keys,
+        prefix_values,
+        routes.T,
+        w_router.T,
         w_out,
         w_gate,
         w_up,

time: 101 us -> 77.1 us (0.76)
  Pallas kernels: 87.8 us -> 72.2 us
  local copies, waits for them, and re-layouts: 6.82 us -> 2.77 us
  other arithmetic: 3.7 us -> 0 us
    pallas_call x1, Pallas kernels: 87.8 us -> 72.2 us  [body(): pl.pallas_call(functools.partial(layer_kernel, n_req, n_tp), out_shape=ja...]
    unnamed x11 -> x1, local copies, waits for them, and re-layouts: 4.5 us -> 1.47 us
    concatenate x2 -> x0, other arithmetic: 2.37 us -> none  [the longest x1 1.75 us: split_router(): return jnp.concatenate(pieces, axis=1)]
    dynamic_slice x2 -> x0, local copies, waits for them, and re-layouts: 1.39 us -> none  [the longest x1 0.75 us: body(): gain = lax.dynamic_slice_in_dim(norm_gain, start, cols, 0).reshape(1, cols)]
    reduce_precision x1 -> x0, other arithmetic: 1.08 us -> none  [split_router(): piece = lax.reduce_precision(rest, 8, 7)]
where the time goes in v2:
time: 77.1 us; the launch traced here: 76.9 us
  Pallas kernels  72.2 us (94%)
  local copies, waits for them, and re-layouts  2.77 us (4%)
  between operations  1.95 us (3%)
    pallas_call x1, Pallas kernels, body(): pl.pallas_call(functools.partial(layer_kernel, n_req, n_tp), out_shape=ja...  72.2 us

profile of v2, /device:TPU:0, one launch (start us, length us, event | category | flops | bytes accessed | tf_op | source)
XLA Modules:
  0.0 76.9 jit_solution(12938670605659384546)
XLA Ops:
  1.9 1.3 %reshape.3.gain = bf16[1,2048]{1,0:T(2,128)(2,1)} reshape(bf16[2048]{0:T(1024)(128)(2,1)} %param.26) | data formatting | bytes 8192 | tf_op jit(solution)/shard_map/reshape | solution.py:625
  3.2 72.2 %shard_map.154 = bf16[64,512]{1,0:T(8,128)(2,1)} custom-call(s32[1]{0:T(128)S(6)} %copy.19.req_group, s32[1]{0:T(128)S(6)} %copy.20.lengths, s32[1]{0:T(128)S(6)} %copy.18.block_group, bf16[64,2048]{1,0:T(8,128)(2,1)} %hidden.1, bf16[1,2048]{1,0:T(2,128)(2,1)} %reshape.3.gain, bf16[64,512]{1,0:T(8,128)(2,1)} %queries.1, bf16[64,512]{1,0:T(8,128)(2,1)} %keys.1, ...), custom_call_target="tpu_custom_call" | custom-call | tf_op jit(solution)/shard_map/pallas_call | solution.py:567
  75.4 1.5 %copy.21 = bf16[64,512]{1,0:T(8,128)(2,1)} copy(bf16[64,512]{1,0:T(8,128)(2,1)} %shard_map.154) | data formatting | bytes 131072
